TPU v7x, 256 devices: a whole 4x4x8 slice. The times are simulated.
256 devices in a mesh: space: 32 (over y, z), chan: 8 (over x, core).
Axes of the slice: x: 4, y: 4, z: 8, core: 2. Of those that a mesh axis runs over, the one named last changes fastest.
Arguments:
- features: bfloat16 [65536, 256], P('space', 'chan'), may hold values from -6 to 6
- kernel_map: int32 [32, 27, 16, 3], P('space'), may hold values from 0 to 31, as said below
- block_count: int32 [32], replicated, may hold values from 3 to 16, as said below
- weight_one: bfloat16 [27, 256, 256], P(None, 'chan'), may hold values from -0.078125 to 0.078125
- weight_two: bfloat16 [27, 256, 256], P(None, 'chan'), may hold values from -0.078125 to 0.078125
- cotangent: bfloat16 [65536, 256], P('space', 'chan'), may hold values from -0.026977539 to 0.026977539
Outputs:
- output: bfloat16 [65536, 256], P('space', 'chan')
- grad_one: float32 [27, 256, 256], P(None, 'chan', 'space')
- grad_two: float32 [27, 256, 256], P(None, 'chan', 'space')
Inputs may be any that keep to these rules, and one draw needn't show every extreme that they name: `kernel_map`: column 0 of slab s's entries is s - 1, s or s + 1. Column 1 is a block below block_count of that source slab; from slab s - 1 it is one of that slab's last 2 live blocks, from slab s + 1 one of its first 2. Column 2 lies below 16. Entries stand in offset order, 16 per offset and slab. `block_count`: at least one slab has all 16 blocks live.
All inputs are finite; a program needn't handle non-finite values.
Results may differ from a plain program's by a relative error of at most 0.015.
Values may be sent and summed in bfloat16 or wider, within the bound.
A program may use at most 64 MiB of HBM per device.

v0:
```python
import jax
import jax.numpy as jnp
from jax import lax
from jax.sharding import PartitionSpec as P

BLK = 128
HB = 2


def padded(shard, sides, width):
    for axis, dim in sides:
        size, length = (lax.axis_size(axis), shard.shape[dim])
        up = [(i, (i + 1) % size) for i in range(size - 1)]
        down = [(j, i) for i, j in up]
        last = lax.slice_in_dim(shard, length - width, length, axis=dim)
        leading = lax.slice_in_dim(shard, 0, width, axis=dim)
        before = lax.ppermute(last, axis, up)
        after = lax.ppermute(leading, axis, down)
        shard = jnp.concatenate([before, shard, after], axis=dim)
    return shard


def local(features, kernel_map, block_count, weight_one, weight_two, cotangent):
    shard = lax.axis_index("space")
    nblocks = features.shape[0] // BLK
    own_count = block_count[shard]
    left_count = block_count[jnp.maximum(shard - 1, 0)]
    entries = kernel_map[0]
    source = entries[..., 0]
    inblock = entries[..., 1]
    target = entries[..., 2]
    position = jnp.where(
        source == shard,
        HB + inblock,
        jnp.where(source < shard, inblock - (left_count - HB), HB + nblocks + inblock),
    )
    live = target < own_count
    select = (target[..., None] == jnp.arange(nblocks, dtype=jnp.int32)) & live[..., None]
    select_f = select.astype(jnp.float32)
    select_b = select.astype(jnp.bfloat16)
    place = (
        (position[..., None] == jnp.arange(nblocks + 2 * HB, dtype=jnp.int32)) & live[..., None]
    ).astype(jnp.float32)

    def widen(feat):
        return lax.all_gather(feat, "chan", axis=1, tiled=True)

    def attach_rims(feat):
        width = feat.shape[1]
        cube = feat.reshape(nblocks, BLK, width)
        first = cube[:HB]
        last = lax.dynamic_slice_in_dim(cube, own_count - HB, HB, 0)
        rims = jnp.concatenate([first, last], 0).reshape(2 * HB * BLK, width)
        outer = padded(rims, (("space", 0),), HB * BLK)
        return jnp.concatenate([outer[: HB * BLK], feat, outer[3 * HB * BLK :]], 0)

    def extend(feat):
        return attach_rims(widen(feat))

    def convolve(wide, weights):
        cube = wide.reshape(-1, BLK, wide.shape[1])

        def convolve_add_offset(total, item):
            index, choose, kernel = item
            picked = cube[index]
            prod = jnp.einsum("erc,dc->erd", picked, kernel, preferred_element_type=jnp.float32)
            return (total + jnp.einsum("eb,erd->brd", choose, prod), None)

        start = jnp.zeros((nblocks, BLK, weights.shape[1]), jnp.float32)
        total, _ = lax.scan(convolve_add_offset, start, (position, select_f, weights))
        return total.reshape(nblocks * BLK, weights.shape[1])

    def weight_grad(wide, grads_cube):
        cube = wide.reshape(-1, BLK, wide.shape[1])

        def one_offset(item):
            index, choose = item
            picked = cube[index]
            chosen = jnp.einsum(
                "eb,brd->erd", choose, grads_cube, preferred_element_type=jnp.float32
            ).astype(jnp.bfloat16)
            return jnp.einsum("erc,erd->dc", picked, chosen, preferred_element_type=jnp.float32)

        return lax.map(one_offset, (position, select_b))

    wide_x = extend(features)
    z_one = convolve(wide_x, weight_one)
    hidden = jax.nn.silu(z_one).astype(jnp.bfloat16)
    wide_h = extend(hidden)
    output = convolve(wide_h, weight_two).astype(jnp.bfloat16)
    grad_cube = cotangent.reshape(nblocks, BLK, -1)
    grad_two = weight_grad(wide_h, grad_cube)
    width = cotangent.shape[1]

    def spread_add_offset(total, item):
        choose, spot, kernel = item
        chosen = jnp.einsum(
            "eb,brd->erd", choose, grad_cube, preferred_element_type=jnp.float32
        ).astype(jnp.bfloat16)
        contrib = jnp.einsum("erd,dc->erc", chosen, kernel, preferred_element_type=jnp.float32)
        return (total + jnp.einsum("ex,erc->xrc", spot, contrib), None)

    start = jnp.zeros((nblocks + 2 * HB, BLK, weight_two.shape[2]), jnp.float32)
    total, _ = lax.scan(spread_add_offset, start, (select_b, place, weight_two))
    partial_value = total.reshape((nblocks + 2 * HB) * BLK, weight_two.shape[2])
    summed = lax.psum_scatter(partial_value, "chan", scatter_dimension=1, tiled=True)
    width = summed.shape[1]
    cube = summed.reshape(-1, BLK, width)
    edges = jnp.concatenate([cube[:HB], cube[HB + nblocks :]], 0).reshape(2 * HB * BLK, width)
    back = padded(edges, (("space", 0),), HB * BLK)
    inner = cube[HB : HB + nblocks]
    from_left = back[: HB * BLK].reshape(HB, BLK, width)
    from_right = back[3 * HB * BLK :].reshape(HB, BLK, width)
    inner = inner.at[:HB].add(from_left)
    tail = lax.dynamic_slice_in_dim(inner, own_count - HB, HB, 0) + from_right
    inner = lax.dynamic_update_slice_in_dim(inner, tail, own_count - HB, 0)
    grad_hidden = inner.reshape(nblocks * BLK, width)
    gate = jax.nn.sigmoid(z_one)
    grad_z = (grad_hidden * gate * (1.0 + z_one * (1.0 - gate))).astype(jnp.bfloat16)
    grad_one = weight_grad(wide_x, grad_z.reshape(nblocks, BLK, -1))
    totals = (
        lax.psum_scatter(grad_one, "space", scatter_dimension=2, tiled=True),
        lax.psum_scatter(grad_two, "space", scatter_dimension=2, tiled=True),
    )
    return (output, totals[0], totals[1])


def solution(mesh):
    return jax.shard_map(
        local,
        mesh=mesh,
        in_specs=(
            P("space", "chan"),
            P("space", None, None, None),
            P(),
            P(None, "chan", None),
            P(None, "chan", None),
            P("space", "chan"),
        ),
        out_specs=(P("space", "chan"), P(None, "chan", "space"), P(None, "chan", "space")),
        check_vma=False,
    )
```

profile of v0, /device:TPU:1, one launch (start us, length us, event | category | flops | bytes accessed | tf_op | source)
XLA Modules:
  0.0 886.4 jit_solution(15789710916156473926)
XLA Ops:
  14.6 25.4 %all-gather.3.cloned.1.call-done = bf16[2048,256]{0,1:T(8,128)(2,1)} async-done(((bf16[2048,32]{0,1:T(8,128)(2,1)}), bf16[2048,256]{0,1:T(8,128)(2,1)}) %all-gather.3.cloned.1.call-update) | async-done | bytes 1048592 | tf_op jit(solution)/shard_map/all_gather | solution.py:46
  41.8 3.2 collective-permute-start
  47.6 3.8 collective-permute-done.1
  55.0 173.4 %while.56 = (s32[]{:T(128)}, f32[16,128,32]{1,0,2:T(8,128)}, bf16[27,16,16]{1,2,0:T(8,128)(2,1)}, s32[27,16]{1,0:T(8,128)S(1)}, bf16[20,128,256]{2,1,0:T(8,128)(...) while((s32[]{:T(128)}, f32[16,128,32]{1,0,2:T(8,128)}, ...), condition=%wide.region_1.2_spmd.clone, body=%wide.region_0.1_spmd.clone.sunk | while | flops 35783728 | bytes 3958115 | solution.py:70
  55.1 2.9 gather_fusion.2
  61.2 2.9 gather_fusion.2
  67.7 2.9 gather_fusion.2
  80.5 2.9 gather_fusion.2
  87.0 2.9 gather_fusion.2
  93.4 2.9 gather_fusion.2
  99.8 2.9 gather_fusion.2
  112.7 2.9 gather_fusion.2
  119.1 2.9 gather_fusion.2
  125.6 2.9 gather_fusion.2
  132.0 2.9 gather_fusion.2
  144.9 2.9 gather_fusion.2
  151.3 2.9 gather_fusion.2
  157.7 2.9 gather_fusion.2
  164.2 2.9 gather_fusion.2
  170.6 2.9 gather_fusion.2
  230.3 108.4 %while.58 = (s32[]{:T(128)}, f32[20,128,256]{2,0,1:T(8,128)S(1)}, bf16[27,16,20]{2,1,0:T(8,128)(2,1)}, bf16[27,16,16]{2,1,0:T(8,128)(2,1)S(1)}, bf16[16,128,32]{...) while((s32[]{:T(128)}, f32[20,128,256]{2,0,1:T(8,128)S(1)}, ...), condition=%wide.region_5.6_spmd.clone, body=%wide.region_4.5_spmd.clone.sunk | while | flops 57999360 | bytes 6317155 | solution.py:104
  341.1 3.2 copy.71
  345.9 3.2 collective-permute-start.2
  351.1 4.9 collective-permute-done.3
  356.1 23.8 %reduce-scatter.10.cloned.1.call-done = f32[32,2560]{1,0:T(8,128)} async-done(((f32[256,2560]{1,0:T(8,128)}), f32[32,2560]{1,0:T(8,128)}) %reduce-scatter.10.cloned.1.call-update) | async-done | bytes 327696
  381.5 3.7 collective-permute-start.4
  388.3 64.0 %while.55 = (s32[]{:T(128)}, f32[27,32,256]{2,1,0:T(8,128)}, bf16[27,16,16]{2,1,0:T(8,128)(2,1)S(1)}, bf16[16,128,32]{1,0,2:T(8,128)(2,1)S(1)}, s32[27,16]{1,0:T...) while((s32[]{:T(128)}, f32[27,32,256]{2,1,0:T(8,128)}, bf16[27,16,16]{2,1,0:T(8,128)(2,1)S(1)}, ...), condition=%wide.region_11.12_spmd, body=%wide.region_10.11_spmd.sunk | while | flops 35718192 | bytes 3580757 | solution.py:84
  452.3 3.4 copy.69
  465.2 141.8 %while.54 = (s32[]{:T(128)}, f32[27,32,256]{2,1,0:T(8,128)}, bf16[27,16,16]{2,1,0:T(8,128)(2,1)}, bf16[16,128,32]{1,0,2:T(8,128)(2,1)S(1)}, s32[27,16]{1,0:T(8,1...) while((s32[]{:T(128)}, f32[27,32,256]{2,1,0:T(8,128)}, bf16[27,16,16]{2,1,0:T(8,128)(2,1)}, ...), condition=%wide.region_8.9_spmd, body=%wide.region_7.8_spmd.sunk | while | flops 35718192 | bytes 3581265 | solution.py:84
  607.0 3.3 copy.68
  610.4 91.2 %while.57 = (s32[]{:T(128)}, f32[16,128,32]{1,0,2:T(8,128)S(1)}, bf16[27,16,16]{1,2,0:T(8,128)(2,1)}, s32[27,16]{1,0:T(8,128)}, bf16[20,128,256]{2,1,0:T(8,128)(...) while((s32[]{:T(128)}, f32[16,128,32]{1,0,2:T(8,128)S(1)}, ...), condition=%wide.region_3.4_spmd.clone, body=%wide.region_2.3_spmd.clone.sunk | while | flops 35783728 | bytes 3958115 | solution.py:70
  702.3 177.6 %reduce-scatter.6.cloned.1.call-done = f32[27,32,8]{1,2,0:T(8,128)} async-done(((f32[27,32,256]{1,2,0:T(8,128)}), f32[27,32,8]{1,2,0:T(8,128)}) %reduce-scatter.6.cloned.1.call-update) | async-done | bytes 27664 | tf_op jit(solution)/shard_map/reduce_scatter | solution.py:122
  (677 shorter events, 564.9 us)
Async XLA Ops:
  7.2 32.8 %all-gather.3.cloned.1.call-start = ((), (), s32[]{:S(2)}) async-start(), calls=%async_computation.3 | async-start | bytes 1179648 | tf_op jit(solution)/shard_map/all_gather | solution.py:46
  7.9 336.5 %all-gather.5.cloned.1.call-start = ((), (), s32[]{:S(2)}) async-start(), calls=%async_computation.4 | async-start | bytes 1179648 | tf_op jit(solution)/shard_map/all_gather | solution.py:46
  40.0 5.0 copy-start.2
  41.8 5.8 collective-permute-start
  45.0 6.4 collective-permute-start.1
  228.5 1.8 copy-start.5
  230.2 149.7 %reduce-scatter.10.cloned.1.call-start = ((), (), s32[]{:S(2)}) async-start(), calls=%async_computation.7 | async-start | bytes 2949120
  344.3 358.0 %reduce-scatter.8.cloned.1.call-start = ((), (), s32[]{:S(2)}) async-start(), calls=%async_computation.6 | async-start | bytes 3649536 | tf_op jit(solution)/shard_map/reduce_scatter | solution.py:123
  345.9 5.2 collective-permute-start.2
  349.2 6.8 collective-permute-start.3
  381.5 78.8 %collective-permute-start.4 = (f32[256,32]{1,0:T(8,128)}, f32[256,32]{1,0:T(8,128)}, u32[]{:S(2)}, u32[]{:S(2)}) collective-permute-start(f32[256,32]{1,0:T(8,128)} %copy.75), channel_id=1, source_target_pairs={{0,8},{8,16},{16,24},{24,32},{32,40},{40,48},{48,56},{56,64},{64,7... | collective-permute-start | bytes 98312 | tf_op jit(solution)/shard_map/ppermute | solution.py:17
  385.9 76.1 %collective-permute-start.5 = (f32[256,32]{1,0:T(8,128)}, f32[256,32]{1,0:T(8,128)}, u32[]{:S(2)}, u32[]{:S(2)}) collective-permute-start(f32[256,32]{1,0:T(8,128)} %copy.76), channel_id=1, source_target_pairs={{8,0},{16,8},{24,16},{32,24},{40,32},{48,40},{56,48},{64,56},{72,6... | collective-permute-start | bytes 98312 | tf_op jit(solution)/shard_map/ppermute | solution.py:18
  452.3 3.4 copy-start.3
  455.7 1.0 copy-start.4
  455.7 8.4 copy-start.1
  455.7 424.2 %reduce-scatter.6.cloned.1.call-start = ((), (), s32[]{:S(2)}) async-start(), calls=%async_computation.5 | async-start | bytes 3649536 | tf_op jit(solution)/shard_map/reduce_scatter | solution.py:122
  456.7 8.6 copy-start
Sparse Core Ops, SparseCore 0:
  9.9 30.0 all-gather.2
  230.4 27.0 all-gather.4
  344.4 35.4 reduce-scatter.9
  455.8 209.5 reduce-scatter.7
  670.3 209.5 reduce-scatter.5
where the time goes:
time: 900 us; the launch traced here: 886 us
  matrix products  331 us (37%)
  waiting for transfers between devices  237 us (26%)
  local copies, waits for them, and re-layouts  223 us (25%)
  other arithmetic  62.2 us (7%)
  between operations  16 us (2%)
  starting transfers between devices  14.2 us (2%)
    reduce_scatter x1, waiting for transfers between devices, local(): lax.psum_scatter(grad_one, 'space', scatter_dimension=2, tiled=True)  178 us
    gather x54, local copies, waits for them, and re-layouts, convolve_add_offset(): picked = cube[index]  96.1 us
    dot_general x54, matrix products, one_offset(): jnp.einsum('erc,erd->dc', picked, chosen, preferred_element_type=jnp.floa...  81.2 us
    dot_general x54, matrix products, convolve_add_offset(): jnp.einsum('erc,dc->erd', picked, kernel, preferred_element_type=jnp.floa...  74.3 us
    dot_general x54, matrix products, convolve_add_offset(): return (total + jnp.einsum('eb,erd->brd', choose, prod), None)  73.9 us
    dot_general x27, matrix products, spread_add_offset(): return (total + jnp.einsum('ex,erc->xrc', spot, contrib), None)  69.9 us
    gather x54, local copies, waits for them, and re-layouts, one_offset(): picked = cube[index]  59.5 us
    select_n x54, other arithmetic, one_offset(): picked = cube[index]  36.8 us
  transfers between devices with their start and end apart: 11, of which 7 were waited for; matrix products, arithmetic and copies ran while one was open for 49% of the time, Pallas kernels for 0%

commit v1 on v0

v1 whole, which is shorter than its diff:
```python
import functools

import jax
import jax.numpy as jnp
from jax import lax
from jax.experimental import pallas as pl
from jax.experimental.pallas import tpu as pltpu
from jax.sharding import PartitionSpec as P

MESH = pl.DeviceIdType.MESH
C = 256
K = 27
BLK = 128
HB = 2
NB = 16
EPK = 16
NX = NB + 2 * HB
NE = K * EPK
NCHAN = 8
NSPACE = 32
D = C // NCHAN
CH = C // NSPACE
KD = K * D
KP = 1024
OWN = NB * BLK
RIM = HB * BLK
EXT = NX * BLK
NSLOT = K * NX
F32 = jnp.float32
BF16 = jnp.bfloat16

T_ROWS = 0
T_SLOTS = NE
T_TEND = 2 * NE
T_SEND = T_TEND + NB
T_LAST = T_SEND + NSLOT


def nt(a, b):
    return lax.dot_general(a, b, (((1,), (1,)), ((), ())), preferred_element_type=F32)


def eye(n):
    row = lax.broadcasted_iota(jnp.int32, (n, n), 0)
    col = lax.broadcasted_iota(jnp.int32, (n, n), 1)
    return jnp.where(row == col, 1.0, 0.0).astype(BF16)


def tables(kernel_map, block_count):
    shard = lax.axis_index("space")
    own = block_count[shard]
    left = block_count[jnp.maximum(shard - 1, 0)]
    entries = kernel_map[0].reshape(NE, 3)
    source, inblock, target = entries[:, 0], entries[:, 1], entries[:, 2]
    pos = jnp.where(
        source == shard,
        inblock,
        jnp.where(source < shard, NB + inblock - (left - HB), NB + HB + inblock),
    )
    live = target < own
    number = jnp.arange(NE, dtype=jnp.int32)
    offset = number // EPK

    def by(key, payload, bits, ends):
        full = key * 512 + number
        rank = jnp.sum((full[None, :] < full[:, None]).astype(jnp.int32), 1)
        value = key * bits + payload
        order = jnp.sum(jnp.where(rank[None, :] == number[:, None], value[None, :], 0), 1)
        keys = order // bits
        same = jnp.concatenate([jnp.zeros((1,), jnp.int32), (keys[1:] == keys[:-1]).astype(jnp.int32)])
        at = jnp.arange(ends, dtype=jnp.int32)[:, None]
        upto = jnp.sum((key[None, :] <= at).astype(jnp.int32), 1)
        there = jnp.sum((key[None, :] == at).astype(jnp.int32), 1)
        return (order % bits, same), (jnp.maximum(upto - 1, 0), (there > 0).astype(jnp.int32))

    rows, tend = by(jnp.where(live, target, NB), pos * K + offset, 1024, NB)
    slots, send = by(jnp.where(live, offset * NX + pos, NSLOT), target, 32, NSLOT)
    last = own - HB + jnp.arange(HB, dtype=jnp.int32)
    which = (last[:, None] == jnp.arange(NB, dtype=jnp.int32)).astype(jnp.int32).reshape(-1)
    index = jnp.concatenate([rows[0], slots[0], tend[0], send[0], last])
    factor = jnp.concatenate([rows[1], slots[1], tend[1], send[1], which])
    return index, factor.astype(F32)


def kernel(
    tab, fac, x_ref, g_ref, w1_ref, w2_ref,
    out_ref, g1_ref, g2_ref,
    xe, he, xrim, hrim, xall, hall, w2t, gblk, zblk, zall, y, run, a_g, a_z, part, got, ghown,
    rimx, rimh, back_out, back_in, gsend1, gsend2, grecv1, grecv2,
    xs, xr, rs, rr, hs, hr, qs, qr, ps, pr, ns, nr, s1s, s1r, s2s, s2r,
):
    chan = lax.axis_index("chan")
    space = lax.axis_index("space")
    right = lax.rem(space + 1, NSPACE)
    left = lax.rem(space + NSPACE - 1, NSPACE)

    barrier = pltpu.get_barrier_semaphore()
    for j in range(1, NCHAN):
        pl.semaphore_signal(
            barrier, inc=1, device_id=(space, lax.rem(chan + j, NCHAN)), device_id_type=MESH
        )

    @pl.loop(1, NSPACE)
    def _(j):
        pl.semaphore_signal(
            barrier, inc=1, device_id=(lax.rem(space + j, NSPACE), chan), device_id_type=MESH
        )

    def remote(src, dst, ssem, rsem, device):
        return pltpu.make_async_remote_copy(
            src_ref=src, dst_ref=dst, send_sem=ssem, recv_sem=rsem, device_id=device, device_id_type=MESH
        )

    mine = pl.ds(pl.multiple_of(chan * D, D), D)

    def gather_copies(own, whole, lanes, ssem, rsem, first):
        return [
            remote(
                own, whole.at[mine, lanes], ssem.at[first + j - 1], rsem.at[first + j - 1],
                (space, lax.rem(chan + j, NCHAN)),
            )
            for j in range(1, NCHAN)
        ]

    def rim_copies(own, last, rim, ssem, rsem):
        return [
            remote(last, rim.at[:, pl.ds(0, RIM)], ssem.at[0], rsem.at[0], (right, chan)),
            remote(own.at[:, pl.ds(0, RIM)], rim.at[:, pl.ds(RIM, RIM)], ssem.at[1], rsem.at[1], (left, chan)),
        ]

    def load_rim(blocks, last):
        for u in range(HB):
            last[:, u * BLK : (u + 1) * BLK] = blocks[tab[T_LAST + u]].astype(BF16)

    body = pl.ds(0, OWN)
    rims = pl.ds(OWN, 2 * RIM)

    ident = eye(D)
    for b in range(0, NB, 4):
        four = nt(ident, x_ref[b * BLK : (b + 4) * BLK, :])
        xe[:, b * BLK : (b + 4) * BLK] = four.astype(BF16)
        for u in range(4):
            gblk[b + u] = four[:, u * BLK : (u + 1) * BLK]
    load_rim(gblk, rimx)

    pl.semaphore_wait(barrier, NCHAN - 1 + NSPACE - 1)

    x_rims = rim_copies(xe, rimx, xrim, rs, rr)
    for copy in x_rims:
        copy.start()
    x_bodies = gather_copies(xe, xall, body, xs, xr, 0)
    for copy in x_bodies:
        copy.start()
    xall[mine, body] = xe[...]

    def scan(src, base):
        def step(i, total):
            for u in range(8):
                n = i * 8 + u
                total = total * fac[base + n] + src[tab[base + n]]
                run[n] = total
            return total

        lax.fori_loop(0, NE // 8, step, jnp.zeros((D, BLK), F32))

    def run_end(at):
        return run[tab[at]] * fac[at]

    def fill_slots(dst):
        @pl.loop(0, K)
        def _(k):
            at = pl.ds(pl.multiple_of(k * D, D), D)
            for p in range(NX):
                dst[at, p * BLK : (p + 1) * BLK] = run_end(T_SEND + k * NX + p).astype(BF16)

    for b in range(0, NB, 4):
        four = nt(ident, g_ref[b * BLK : (b + 4) * BLK, :])
        for u in range(4):
            gblk[b + u] = four[:, u * BLK : (u + 1) * BLK]
    a_g[KD:, :] = jnp.zeros((KP - KD, EXT), BF16)
    a_z[KD:, :] = jnp.zeros((KP - KD, EXT), BF16)
    w2t[:, KD:] = jnp.zeros((C, KP - KD), BF16)
    w2t[:, :KD] = nt(eye(C), w2_ref[...]).astype(BF16)
    scan(gblk, T_SLOTS)
    fill_slots(a_g)

    for copy in x_rims:
        copy.wait_recv()
    x_sides = gather_copies(xrim, xall, rims, xs, xr, NCHAN - 1)
    for copy in x_sides:
        copy.start()
    xall[mine, rims] = xrim[...]

    @pl.loop(0, NX // 2)
    def _(p):
        two = pl.ds(pl.multiple_of(p * 2 * BLK, 2 * BLK), 2 * BLK)
        part[:, two] = jnp.dot(w2t[...], a_g[:, two], preferred_element_type=F32).astype(BF16)

    p_copies = []
    for j in range(1, NCHAN):
        to = lax.rem(chan + j, NCHAN)
        p_copies.append(
            remote(
                part.at[pl.ds(pl.multiple_of(to * D, D), D), :], got.at[j - 1],
                ps.at[j - 1], pr.at[j - 1], (space, to),
            )
        )
    for copy in p_copies:
        copy.start()

    def products(w_ref, whole):
        @pl.loop(0, NX // 2)
        def _(p):
            two = pl.ds(pl.multiple_of(p * 2 * BLK, 2 * BLK), 2 * BLK)
            prod = jnp.dot(w_ref[...], whole[:, two], preferred_element_type=F32)
            y[pl.ds(p * 2 * K, K)] = prod[:, :BLK].reshape(K, D, BLK)
            y[pl.ds(p * 2 * K + K, K)] = prod[:, BLK:].reshape(K, D, BLK)

    for copy in x_bodies + x_sides:
        copy.wait_recv()
    products(w1_ref, xall)
    scan(y, T_ROWS)
    for b in range(NB):
        z = run_end(T_TEND + b)
        zblk[b] = z
        h = z / (1.0 + jnp.exp(-z))
        gblk[b] = h
        he[:, b * BLK : (b + 1) * BLK] = h.astype(BF16)
    load_rim(gblk, rimh)
    h_rims = rim_copies(he, rimh, hrim, qs, qr)
    for copy in h_rims:
        copy.start()
    h_bodies = gather_copies(he, hall, body, hs, hr, 0)
    for copy in h_bodies:
        copy.start()
    hall[mine, body] = he[...]

    for copy in p_copies:
        copy.wait_recv()
    for p in range(0, NX, 4):
        at = pl.ds(p * BLK, 4 * BLK)
        total = part[mine, at].astype(F32)
        for j in range(NCHAN - 1):
            total = total + got[j, :, at].astype(F32)
        ghown[:, at] = total
    back_out[0] = ghown[:, OWN : OWN + RIM]
    back_out[1] = ghown[:, OWN + RIM :]
    n_copies = [
        remote(back_out.at[0], back_in.at[0], ns.at[0], nr.at[0], (left, chan)),
        remote(back_out.at[1], back_in.at[1], ns.at[1], nr.at[1], (right, chan)),
    ]
    for copy in n_copies:
        copy.start()
    for copy in h_rims:
        copy.wait_recv()
    h_sides = gather_copies(hrim, hall, rims, hs, hr, NCHAN - 1)
    for copy in h_sides:
        copy.start()
    hall[mine, rims] = hrim[...]
    for copy in n_copies:
        copy.wait_recv()
    for b in range(NB):
        grad = ghown[:, b * BLK : (b + 1) * BLK]
        if b < HB:
            grad = grad + back_in[1, :, b * BLK : (b + 1) * BLK]
        for u in range(HB):
            grad = grad + back_in[0, :, u * BLK : (u + 1) * BLK] * fac[T_LAST + u * NB + b]
        z = zblk[b]
        gate = 1.0 / (1.0 + jnp.exp(-z))
        grad_z = grad * gate * (1.0 + z * (1.0 - gate))
        gblk[b] = grad_z.astype(BF16).astype(F32)
    scan(gblk, T_SLOTS)
    fill_slots(a_z)

    def kernel_grad(whole, a, gsend, grecv, ssem, rsem):
        for n in range(4):
            prod = nt(whole[...], a[n * 256 : (n + 1) * 256, :])
            rows, lanes = (n // 2) * CH, slice((n % 2) * 256, (n % 2) * 256 + 256)
            zall[:, rows : rows + CH, lanes] = prod.reshape(NSPACE, CH, 256)
        gsend[...] = zall[...].astype(BF16)

        @pl.loop(1, NSPACE)
        def _(j):
            to = lax.rem(space + j, NSPACE)
            remote(gsend.at[to], grecv.at[j - 1], ssem.at[j - 1], rsem.at[j - 1], (to, chan)).start()

    def collect(gsend, grecv, ssem, rsem, dst):
        def step(j, total):
            to = lax.rem(space + j, NSPACE)
            remote(gsend.at[to], grecv.at[j - 1], ssem.at[j - 1], rsem.at[j - 1], (to, chan)).wait()
            return total + grecv[j - 1].astype(F32)

        total = lax.fori_loop(1, NSPACE, step, gsend[space].astype(F32))
        dst[: KP // 2, :] = jnp.transpose(total[:CH, :])
        dst[KP // 2 :, :] = jnp.transpose(total[CH:, :])[: KD - KP // 2, :]

    kernel_grad(xall, a_z, gsend1, grecv1, s1s, s1r)

    for copy in h_bodies + h_sides:
        copy.wait_recv()
    kernel_grad(hall, a_g, gsend2, grecv2, s2s, s2r)
    products(w2_ref, hall)
    scan(y, T_ROWS)
    for b in range(NB):
        z = run_end(T_TEND + b)
        out_ref[b * BLK : (b + 1) * BLK, :] = jnp.transpose(z).astype(BF16)

    collect(gsend1, grecv1, s1s, s1r, g1_ref)
    collect(gsend2, grecv2, s2s, s2r, g2_ref)
    for copy in x_rims + x_bodies + x_sides + p_copies + h_rims + h_bodies + h_sides + n_copies:
        copy.wait_send()


def local(features, kernel_map, block_count, weight_one, weight_two, cotangent):
    index, factor = tables(kernel_map, block_count)
    vmem = pl.BlockSpec(memory_space=pltpu.VMEM)
    dma = pltpu.SemaphoreType.DMA
    output, one, two = pl.pallas_call(
        kernel,
        out_shape=(
            jax.ShapeDtypeStruct((OWN, D), BF16),
            jax.ShapeDtypeStruct((KD, CH), F32),
            jax.ShapeDtypeStruct((KD, CH), F32),
        ),
        in_specs=[pl.BlockSpec(memory_space=pltpu.SMEM)] * 2 + [vmem] * 4,
        out_specs=(vmem,) * 3,
        scratch_shapes=[
            pltpu.VMEM((D, OWN), BF16),
            pltpu.VMEM((D, OWN), BF16),
            pltpu.VMEM((D, 2 * RIM), BF16),
            pltpu.VMEM((D, 2 * RIM), BF16),
            pltpu.VMEM((C, EXT), BF16),
            pltpu.VMEM((C, EXT), BF16),
            pltpu.VMEM((C, KP), BF16),
            pltpu.VMEM((NB, D, BLK), F32),
            pltpu.VMEM((NB, D, BLK), F32),
            pltpu.VMEM((NSPACE, 2 * CH, KP // 2), F32),
            pltpu.VMEM((NSLOT, D, BLK), F32),
            pltpu.VMEM((NE, D, BLK), F32),
            pltpu.VMEM((KP, EXT), BF16),
            pltpu.VMEM((KP, EXT), BF16),
            pltpu.VMEM((C, EXT), BF16),
            pltpu.VMEM((NCHAN - 1, D, EXT), BF16),
            pltpu.VMEM((D, EXT), F32),
            pltpu.VMEM((D, RIM), BF16),
            pltpu.VMEM((D, RIM), BF16),
            pltpu.VMEM((2, D, RIM), F32),
            pltpu.VMEM((2, D, RIM), F32),
            pltpu.VMEM((NSPACE, 2 * CH, KP // 2), BF16),
            pltpu.VMEM((NSPACE, 2 * CH, KP // 2), BF16),
            pltpu.VMEM((NSPACE - 1, 2 * CH, KP // 2), BF16),
            pltpu.VMEM((NSPACE - 1, 2 * CH, KP // 2), BF16),
            dma((2 * NCHAN - 2,)),
            dma((2 * NCHAN - 2,)),
            dma((2,)),
            dma((2,)),
            dma((2 * NCHAN - 2,)),
            dma((2 * NCHAN - 2,)),
            dma((2,)),
            dma((2,)),
            dma((NCHAN - 1,)),
            dma((NCHAN - 1,)),
            dma((2,)),
            dma((2,)),
            dma((NSPACE - 1,)),
            dma((NSPACE - 1,)),
            dma((NSPACE - 1,)),
            dma((NSPACE - 1,)),
        ],
        compiler_params=pltpu.CompilerParams(
            collective_id=0, has_side_effects=True, vmem_limit_bytes=56 * 2**20
        ),
    )(index, factor, features, cotangent, weight_one.reshape(KD, C), weight_two.reshape(KD, C))
    return output, one.reshape(K, D, CH), two.reshape(K, D, CH)


def solution(mesh):
    return jax.shard_map(
        local,
        mesh=mesh,
        in_specs=(
            P("space", "chan"),
            P("space", None, None, None),
            P(),
            P(None, "chan", None),
            P(None, "chan", None),
            P("space", "chan"),
        ),
        out_specs=(P("space", "chan"), P(None, "chan", "space"), P(None, "chan", "space")),
        check_vma=False,
    )
```

time: 900 us -> 95.1 us (0.11); the launches traced: 886 us -> 94.8 us
  matrix products: 331 us -> 0 us
  waiting for transfers between devices: 237 us -> 0 us
  local copies, waits for them, and re-layouts: 223 us -> 9.63 us
  Pallas kernels: 0 us -> 79 us
  other arithmetic: 62.2 us -> 4.1 us
  starting transfers between devices: 14.2 us -> 0 us
  between operations: 16 us -> 2.07 us
    dot_general x270 -> x0, matrix products: 331 us -> none  [the longest x54 81.2 us: one_offset(): jnp.einsum('erc,erd->dc', picked, chosen, preferred_element_type=jnp.floa...]
    reduce_scatter x2 -> x0, waiting for transfers between devices: 178 us -> none  [the longest x1 178 us: local(): lax.psum_scatter(grad_one, 'space', scatter_dimension=2, tiled=True)]
    gather x108 -> x0, local copies, waits for them, and re-layouts: 156 us -> none  [the longest x54 96.1 us: convolve_add_offset(): picked = cube[index]]
    pallas_call x0 -> x1, Pallas kernels: none -> 79 us  [local(): pl.pallas_call(kernel, out_shape=(jax.ShapeDtypeStruct((OWN, D), BF16), j...]
    select_n x109 -> x2, other arithmetic: 55.5 us -> 0.02 us  [by(): keys = order // bits]
    convert_element_type x27 -> x1, local copies, waits for them, and re-layouts: 33.4 us -> 0.09 us  [tables(): (last[:, None] == jnp.arange(NB, dtype=jnp.int32)).astype(jnp.int32)]
    all_gather x2 -> x0, waiting for transfers between devices: 25.4 us -> none  [widen(): return lax.all_gather(feat, 'chan', axis=1, tiled=True)]
    unnamed x6 -> x0, waiting for transfers between devices: 24.6 us -> none
  transfers between devices with their start and end apart: 11 -> 0, of which waited for: 7 -> 0; matrix products, arithmetic and copies ran while one was open for 49% -> 0% of each run, Pallas kernels for 0% -> 0%
where the time goes in v1:
time: 95.1 us; the launch traced here: 94.8 us
  Pallas kernels  79 us (83%)
  local copies, waits for them, and re-layouts  9.63 us (10%)
  other arithmetic  4.1 us (4%)
  between operations  2.07 us (2%)
    pallas_call x1, Pallas kernels, local(): pl.pallas_call(kernel, out_shape=(jax.ShapeDtypeStruct((OWN, D), BF16), j...  79 us
    unnamed x12, local copies, waits for them, and re-layouts  7.36 us
    add x3, other arithmetic, by(): full = key * 512 + number  1.97 us

profile of v1, /device:TPU:1, one launch (start us, length us, event | category | flops | bytes accessed | tf_op | source)
XLA Modules:
  0.0 94.8 jit_solution(2997205266750837267)
XLA Ops:
  0.6 0.0 copy-start.2
  0.6 1.3 %fusion.13 = (s32[1]{0:T(128)}, s32[1]{0:T(128)}) fusion(s32[32]{0:T(128)} %param.8, s32[]{:T(128)S(6)} %max.9, s32[]{:T(128)S(6)} %select_n.128), kind=kLoop, calls=%fused_computation.71 | loop fusion | bytes 24 | tf_op jit(solution)/shard_map/dynamic_slice | solution.py:52
  3.3 0.1 iota_compare_fusion.6
  3.4 0.1 convert_element_type.36
  3.4 0.8 copy.20
  4.3 0.1 reshape_squeeze.3
  4.4 0.7 iota_add_fusion
  5.1 0.7 iota_add_fusion.2
  5.7 0.3 convert_reduce_fusion.3
  6.0 0.1 convert_reduce_fusion.4
  6.1 0.7 iota_add_fusion.1
  6.8 0.4 convert_reduce_fusion.2
  7.2 0.2 select_reduce_fusion
  7.4 0.1 slice_compare_fusion
  7.5 0.1 slice_compare_fusion.1
  7.5 0.3 convert_reduce_fusion
  7.9 0.1 concatenate.10
  8.0 0.7 concatenate.9.tab
  8.6 0.6 convert_convert_fusion.fac
  9.2 1.9 %copy.21.x_ref = bf16[2048,32]{1,0:T(8,128)(2,1)} copy(bf16[2048,32]{0,1:T(8,128)(2,1)} %param.6) | data formatting | bytes 262144 | tf_op args[0]
  11.1 0.0 copy-done.2
  11.1 1.0 %copy.22.g_ref = bf16[2048,32]{1,0:T(8,128)(2,1)} copy(bf16[2048,32]{0,1:T(8,128)(2,1)S(1)} %copy-done.2) | data formatting | bytes 262144 | tf_op args[5]
  12.2 79.0 %shard_map.85 = (bf16[2048,32]{1,0:T(8,128)(2,1)}, f32[864,8]{1,0:T(8,128)}, f32[864,8]{1,0:T(8,128)}) custom-call(s32[1422]{0:T(1024)} %concatenate.9.tab, f32[1452]{0:T(1024)} %convert_convert_fusion.fac, bf16[2048,32]{1,0:T(8,128)(2,1)} %copy.21.x_ref, bf16[2048,32]{1,0:T(8,128)(2,1)} %copy.22.g_ref, bf16[864,256]{1,0:T(8,128)(2,1)} %bitcast.14, ...), custom_call_target="tpu_custom_call" | custom-call | tf_op jit(solution)/shard_map/pallas_call | solution.py:318
  91.2 0.0 copy-start.1
  91.2 0.0 copy-start
  91.2 2.0 %copy.23 = bf16[2048,32]{0,1:T(8,128)(2,1)} copy(bf16[2048,32]{1,0:T(8,128)(2,1)} %get-tuple-element.15) | data formatting | bytes 262144
  93.1 0.0 copy-done.1
  93.1 0.8 copy.24
  94.0 0.0 copy-done
  94.0 0.8 copy.25
  (9 shorter events, 0.1 us)
Async XLA Ops:
  0.6 10.5 %copy-start.2 = (bf16[2048,32]{0,1:T(8,128)(2,1)S(1)}, bf16[2048,32]{0,1:T(8,128)(2,1)}, u32[]{:S(2)}) copy-start(bf16[2048,32]{0,1:T(8,128)(2,1)} %param.11) | copy-start | bytes 393220
  91.2 2.0 %copy-start.1 = (f32[864,8]{1,0:T(8,128)S(1)}, f32[864,8]{1,0:T(8,128)}, u32[]{:S(2)}) copy-start(f32[864,8]{1,0:T(8,128)} %get-tuple-element.7) | copy-start | bytes 82948
  91.2 2.8 %copy-start = (f32[864,8]{1,0:T(8,128)S(1)}, f32[864,8]{1,0:T(8,128)}, u32[]{:S(2)}) copy-start(f32[864,8]{1,0:T(8,128)} %get-tuple-element.8) | copy-start | bytes 82948

commit v2 on v1

v2 whole, which is shorter than its diff:
```python
import jax
import jax.numpy as jnp
from jax import lax
from jax.experimental import pallas as pl
from jax.experimental.pallas import tpu as pltpu
from jax.sharding import PartitionSpec as P

MESH = pl.DeviceIdType.MESH
C = 256
K = 27
BLK = 128
HB = 2
NB = 16
EPK = 16
NX = NB + 2 * HB
NE = K * EPK
NCHAN = 8
NSPACE = 32
D = C // NCHAN
CH = C // NSPACE
KD = K * D
KP = 896
KW = 512
NY = 4
NZ = NSPACE // NY
CY = C // NY
OWN = NB * BLK
RIM = HB * BLK
EXT = NX * BLK
NSLOT = K * NX
F32 = jnp.float32
BF16 = jnp.bfloat16

T_ROWS = 0
T_SLOTS = NE
T_TEND = 2 * NE
T_SEND = T_TEND + NB
T_LAST = T_SEND + NSLOT


def nt(a, b):
    return lax.dot_general(a, b, (((1,), (1,)), ((), ())), preferred_element_type=F32)


def eye(n):
    row = lax.broadcasted_iota(jnp.int32, (n, n), 0)
    col = lax.broadcasted_iota(jnp.int32, (n, n), 1)
    return jnp.where(row == col, 1.0, 0.0).astype(BF16)


def by_core():
    row = lax.broadcasted_iota(jnp.int32, (C, C), 0)
    col = lax.broadcasted_iota(jnp.int32, (C, C), 1)
    core, rest = row // (C // 2), row % (C // 2)
    return jnp.where(col == (rest // D) * (2 * D) + core * D + rest % D, 1.0, 0.0).astype(BF16)


def tables(kernel_map, block_count):
    shard = lax.axis_index("space")
    own = block_count[shard]
    left = block_count[jnp.maximum(shard - 1, 0)]
    entries = kernel_map[0].reshape(NE, 3)
    source, inblock, target = entries[:, 0], entries[:, 1], entries[:, 2]
    pos = jnp.where(
        source == shard,
        inblock,
        jnp.where(source < shard, NB + inblock - (left - HB), NB + HB + inblock),
    )
    live = target < own
    number = jnp.arange(NE, dtype=jnp.int32)
    offset = number // EPK

    def by(key, payload, bits, ends):
        full = key * 512 + number
        rank = jnp.sum((full[None, :] < full[:, None]).astype(jnp.int32), 1)
        value = key * bits + payload
        order = jnp.sum(jnp.where(rank[None, :] == number[:, None], value[None, :], 0), 1)
        keys = order // bits
        same = jnp.concatenate([jnp.zeros((1,), jnp.int32), (keys[1:] == keys[:-1]).astype(jnp.int32)])
        at = jnp.arange(ends, dtype=jnp.int32)[:, None]
        upto = jnp.sum((key[None, :] <= at).astype(jnp.int32), 1)
        there = jnp.sum((key[None, :] == at).astype(jnp.int32), 1)
        return (order % bits, same), (jnp.maximum(upto - 1, 0), (there > 0).astype(jnp.int32))

    rows, tend = by(jnp.where(live, target, NB), pos * K + offset, 1024, NB)
    slots, send = by(jnp.where(live, offset * NX + pos, NSLOT), target, 32, NSLOT)
    last = own - HB + jnp.arange(HB, dtype=jnp.int32)
    which = (last[:, None] == jnp.arange(NB, dtype=jnp.int32)).astype(jnp.int32).reshape(-1)
    index = jnp.concatenate([rows[0], slots[0], tend[0], send[0], last])
    factor = jnp.concatenate([rows[1], slots[1], tend[1], send[1], which])
    return index, factor.astype(F32)


def kernel(
    tab, fac, x_ref, g_ref, w1_ref, w2_ref,
    out_ref, g1_ref, g2_ref,
    xall, hall, xlast, xrim, hlast, hrim, w2t, blocks, zblk, y, run, a_g, a_z,
    part, sibp, comb, via, came, ghown, back_out, back_in,
    ysend1, ysend2, yrecv1, yrecv2, wide, zsend1, zsend2, zrecv1, zrecv2,
    xs, xr, rs, rr, hs, hr, qs, qr, bs, br, cs, cr, ns, nr,
    y1s, y1r, y2s, y2r, z1s, z1r, z2s, z2r,
):
    chan = lax.axis_index("chan")
    space = lax.axis_index("space")
    core = lax.rem(chan, 2)
    chip = chan // 2
    sib = chan + 1 - 2 * core
    ahead = lax.rem(chan + 2, NCHAN)
    behind = lax.rem(chan + NCHAN - 2, NCHAN)
    opposite = lax.rem(chan + NCHAN // 2, NCHAN)
    right = lax.rem(space + 1, NSPACE)
    left = lax.rem(space + NSPACE - 1, NSPACE)
    row = space // NZ
    col = lax.rem(space, NZ)

    def along_y(j):
        return lax.rem(space + j * NZ, NSPACE)

    def along_z(j):
        return row * NZ + lax.rem(col + j, NZ)

    peers = [(space, sib), (space, ahead), (space, behind), (right, chan), (left, chan)]
    peers += [(along_y(j), chan) for j in range(1, NY)] + [(along_z(j), chan) for j in range(1, NZ)]
    barrier = pltpu.get_barrier_semaphore()
    for peer in peers:
        pl.semaphore_signal(barrier, inc=1, device_id=peer, device_id_type=MESH)

    def remote(src, dst, ssem, rsem, device):
        return pltpu.make_async_remote_copy(
            src_ref=src, dst_ref=dst, send_sem=ssem, recv_sem=rsem, device_id=device, device_id_type=MESH
        )

    def channels(who):
        return pl.ds(pl.multiple_of(who * D, D), D)

    mine = channels(chan)
    body = pl.ds(0, OWN)
    rims = pl.ds(OWN, 2 * RIM)
    pending = []

    def start(copy):
        copy.start()
        pending.append(copy)

    class Gather:
        def __init__(self, whole, ssem, rsem):
            half = OWN // 2
            lanes = [pl.ds(0, half), pl.ds(half, half), pl.ds(OWN, RIM), pl.ds(OWN + RIM, RIM)]
            ways = [(chan, ahead), (chan, behind), (chan, sib), None, (behind, sib), (ahead, sib), (opposite, sib)]
            self.copy = {}
            for kind, way in enumerate(ways):
                for p in range(4):
                    origin, to = way or ((behind, ahead), (ahead, behind))[p % 2]
                    ref = whole.at[channels(origin), lanes[p]]
                    n = kind * 4 + p
                    self.copy[kind, p] = remote(ref, ref, ssem.at[n], rsem.at[n], (space, to))

        def send(self, parts):
            for kind in range(3):
                for p in parts:
                    start(self.copy[kind, p])

        def relay(self, parts):
            for p in parts:
                for kind in (0, 1):
                    self.copy[kind, p].wait_recv()
                    if p % 2 == kind:
                        start(self.copy[3, p])
                    start(self.copy[4 + kind, p])

        def finish(self, parts):
            for p in parts:
                self.copy[3, p].wait_recv()
                start(self.copy[6, p])
            for p in parts:
                for kind in (2, 4, 5, 6):
                    self.copy[kind, p].wait_recv()

    def rim_copies(whole, last, rim, ssem, rsem):
        return [
            remote(last, rim.at[:, pl.ds(0, RIM)], ssem.at[0], rsem.at[0], (right, chan)),
            remote(whole.at[mine, pl.ds(0, RIM)], rim.at[:, pl.ds(RIM, RIM)], ssem.at[1], rsem.at[1], (left, chan)),
        ]

    def load_last(last):
        for u in range(HB):
            last[:, u * BLK : (u + 1) * BLK] = blocks[tab[T_LAST + u]].astype(BF16)

    ident = eye(D)
    for b in range(0, NB, 4):
        four = nt(ident, x_ref[b * BLK : (b + 4) * BLK, :])
        xall[mine, b * BLK : (b + 4) * BLK] = four.astype(BF16)
        for u in range(4):
            blocks[b + u] = four[:, u * BLK : (u + 1) * BLK]
    load_last(xlast)

    pl.semaphore_wait(barrier, len(peers))

    x_rims = rim_copies(xall, xlast, xrim, rs, rr)
    for copy in x_rims:
        start(copy)
    x_all = Gather(xall, xs, xr)
    x_all.send((0, 1))

    def scan(src, base):
        def step(i, total):
            for u in range(8):
                n = i * 8 + u
                total = total * fac[base + n] + src[tab[base + n]]
                run[n] = total
            return total

        lax.fori_loop(0, NE // 8, step, jnp.zeros((D, BLK), F32))

    def run_end(at):
        return run[tab[at]] * fac[at]

    def fill_slots(dst):
        @pl.loop(0, K)
        def _(k):
            at = pl.ds(pl.multiple_of(k * D, D), D)
            for p in range(NX):
                dst[at, p * BLK : (p + 1) * BLK] = run_end(T_SEND + k * NX + p).astype(BF16)

    for b in range(0, NB, 4):
        four = nt(ident, g_ref[b * BLK : (b + 4) * BLK, :])
        for u in range(4):
            blocks[b + u] = four[:, u * BLK : (u + 1) * BLK]
    a_g[KD:, :] = jnp.zeros((KP - KD, EXT), BF16)
    a_z[KD:, :] = jnp.zeros((KP - KD, EXT), BF16)
    w2t[:, KD:] = jnp.zeros((C, KP - KD), BF16)
    for copy in x_rims:
        copy.wait_recv()
    xall[mine, rims] = xrim[...]
    x_all.send((2, 3))
    w2t[:, :KD] = nt(by_core(), w2_ref[...]).astype(BF16)
    scan(blocks, T_SLOTS)
    x_all.relay((0, 1))
    fill_slots(a_g)
    x_all.relay((2, 3))

    theirs = pl.ds(pl.multiple_of((1 - core) * (C // 2), C // 2), C // 2)
    ours = pl.ds(pl.multiple_of(core * (C // 2), C // 2), C // 2)
    halves = [pl.ds(0, EXT // 2), pl.ds(EXT // 2, EXT // 2)]
    to_sib = [remote(part.at[theirs, h], sibp.at[:, h], bs.at[i], br.at[i], (space, sib)) for i, h in enumerate(halves)]
    for i in range(2):

        @pl.loop(i * NX // 4, (i + 1) * NX // 4)
        def _(p):
            two = pl.ds(pl.multiple_of(p * 2 * BLK, 2 * BLK), 2 * BLK)
            part[:, two] = jnp.dot(w2t[...], a_g[:, two], preferred_element_type=F32).astype(BF16)

        start(to_sib[i])

    def products(w_ref, whole):
        @pl.loop(0, NX // 2)
        def _(p):
            two = pl.ds(pl.multiple_of(p * 2 * BLK, 2 * BLK), 2 * BLK)
            prod = jnp.dot(w_ref[...], whole[:, two], preferred_element_type=F32)
            y[pl.ds(p * 2 * K, K)] = prod[:, :BLK].reshape(K, D, BLK)
            y[pl.ds(p * 2 * K + K, K)] = prod[:, BLK:].reshape(K, D, BLK)

    x_all.finish((0, 1, 2, 3))
    products(w1_ref, xall)

    def rows_for(chips):
        return pl.ds(pl.multiple_of(lax.rem(chip + chips, NCHAN // 2) * D, D), D)

    to_ahead = [
        remote(comb.at[rows_for(2), halves[0]], via.at[0], cs.at[0], cr.at[0], (space, ahead)),
        remote(comb.at[rows_for(1), halves[1]], came.at[0, :, halves[1]], cs.at[1], cr.at[1], (space, ahead)),
        remote(comb.at[rows_for(1), halves[0]], came.at[0, :, halves[0]], cs.at[2], cr.at[2], (space, ahead)),
    ]
    to_behind = [
        remote(comb.at[rows_for(2), halves[1]], via.at[1], cs.at[3], cr.at[3], (space, behind)),
        remote(comb.at[rows_for(3), halves[0]], came.at[1, :, halves[0]], cs.at[4], cr.at[4], (space, behind)),
        remote(comb.at[rows_for(3), halves[1]], came.at[1, :, halves[1]], cs.at[5], cr.at[5], (space, behind)),
    ]
    for i, h in enumerate(halves):
        to_sib[i].wait_recv()
        comb[:, h] = (part[ours, h].astype(F32) + sibp[:, h].astype(F32)).astype(BF16)
    for i in range(2):
        start(to_ahead[i])
        start(to_behind[i])

    scan(y, T_ROWS)
    to_ahead[0].wait_recv()
    comb[rows_for(1), halves[0]] = (comb[rows_for(1), halves[0]].astype(F32) + via[0].astype(F32)).astype(BF16)
    start(to_ahead[2])
    to_behind[0].wait_recv()
    comb[rows_for(3), halves[1]] = (comb[rows_for(3), halves[1]].astype(F32) + via[1].astype(F32)).astype(BF16)
    start(to_behind[2])

    for b in range(NB):
        z = run_end(T_TEND + b)
        zblk[b] = z
        h = z / (1.0 + jnp.exp(-z))
        blocks[b] = h
        hall[mine, b * BLK : (b + 1) * BLK] = h.astype(BF16)
    load_last(hlast)
    h_rims = rim_copies(hall, hlast, hrim, qs, qr)
    for copy in h_rims:
        start(copy)
    h_all = Gather(hall, hs, hr)
    h_all.send((0, 1))

    for copy in to_ahead[1:] + to_behind[1:]:
        copy.wait_recv()
    for p in range(0, NX, 4):
        at = pl.ds(p * BLK, 4 * BLK)
        ghown[:, at] = comb[rows_for(0), at].astype(F32) + came[0, :, at].astype(F32) + came[1, :, at].astype(F32)
    back_out[0] = ghown[:, OWN : OWN + RIM]
    back_out[1] = ghown[:, OWN + RIM :]
    n_copies = [
        remote(back_out.at[0], back_in.at[0], ns.at[0], nr.at[0], (left, chan)),
        remote(back_out.at[1], back_in.at[1], ns.at[1], nr.at[1], (right, chan)),
    ]
    for copy in n_copies:
        start(copy)
    for copy in h_rims:
        copy.wait_recv()
    hall[mine, rims] = hrim[...]
    h_all.send((2, 3))
    for copy in n_copies:
        copy.wait_recv()
    for b in range(NB):
        grad = ghown[:, b * BLK : (b + 1) * BLK]
        if b < HB:
            grad = grad + back_in[1, :, b * BLK : (b + 1) * BLK]
        for u in range(HB):
            grad = grad + back_in[0, :, u * BLK : (u + 1) * BLK] * fac[T_LAST + u * NB + b]
        z = zblk[b]
        gate = 1.0 / (1.0 + jnp.exp(-z))
        grad_z = grad * gate * (1.0 + z * (1.0 - gate))
        blocks[b] = grad_z.astype(BF16).astype(F32)
    h_all.relay((0, 1))
    scan(blocks, T_SLOTS)
    h_all.relay((2, 3))
    fill_slots(a_z)

    class Sum:
        def __init__(self, ysend, yrecv, zsend, zrecv, ys, yr, zs, zr):
            self.ysend, self.yrecv, self.zsend, self.zrecv = ysend, yrecv, zsend, zrecv
            self.over_y, self.over_z = [], []
            for j in range(1, NY):
                at = pl.ds(pl.multiple_of(lax.rem(row + j, NY) * CY, CY), CY)
                self.over_y.append(
                    remote(ysend.at[at], yrecv.at[j - 1], ys.at[j - 1], yr.at[j - 1], (along_y(j), chan))
                )
            for j in range(1, NZ):
                to = lax.rem(col + j, NZ)
                self.over_z.append(
                    remote(zsend.at[to], zrecv.at[j - 1], zs.at[j - 1], zr.at[j - 1], (along_z(j), chan))
                )

        def begin(self, whole, a):
            for n in range(0, KP, 256):
                at = slice(n, min(n + 256, KP))
                self.ysend[:, at] = nt(whole[...], a[at, :]).astype(BF16)
            for copy in self.over_y:
                start(copy)

        def middle(self):
            for copy in self.over_y:
                copy.wait_recv()
            own = self.ysend[pl.ds(pl.multiple_of(row * CY, CY), CY), :].astype(F32)
            for j in range(NY - 1):
                own = own + self.yrecv[j].astype(F32)
            wide[:, :CH, :] = own[:, :KW].reshape(NZ, CH, KW)
            wide[:, CH:, : KP - KW] = own[:, KW:].reshape(NZ, CH, KP - KW)
            wide[:, CH:, KP - KW :] = jnp.zeros((NZ, CH, 2 * KW - KP), F32)
            self.zsend[...] = wide[...].astype(BF16)
            for copy in self.over_z:
                start(copy)

        def end(self, dst):
            total = self.zsend[col].astype(F32)
            for j, copy in enumerate(self.over_z):
                copy.wait_recv()
                total = total + self.zrecv[j].astype(F32)
            dst[:KW, :] = jnp.transpose(total[:CH, :])
            dst[KW:, :] = jnp.transpose(total[CH:, :])[: KD - KW, :]

    one = Sum(ysend1, yrecv1, zsend1, zrecv1, y1s, y1r, z1s, z1r)
    two = Sum(ysend2, yrecv2, zsend2, zrecv2, y2s, y2r, z2s, z2r)
    one.begin(xall, a_z)

    h_all.finish((0, 1, 2, 3))
    two.begin(hall, a_g)
    one.middle()
    products(w2_ref, hall)
    two.middle()
    scan(y, T_ROWS)
    for b in range(NB):
        z = run_end(T_TEND + b)
        out_ref[b * BLK : (b + 1) * BLK, :] = jnp.transpose(z).astype(BF16)
    one.end(g1_ref)
    two.end(g2_ref)
    for copy in pending:
        copy.wait_send()


def local(features, kernel_map, block_count, weight_one, weight_two, cotangent):
    index, factor = tables(kernel_map, block_count)
    vmem = pl.BlockSpec(memory_space=pltpu.VMEM)

    def v(shape, kind=BF16):
        return pltpu.VMEM(shape, kind)

    def dma(n):
        return [pltpu.SemaphoreType.DMA((n,))] * 2

    output, one, two = pl.pallas_call(
        kernel,
        out_shape=(
            jax.ShapeDtypeStruct((OWN, D), BF16),
            jax.ShapeDtypeStruct((KD, CH), F32),
            jax.ShapeDtypeStruct((KD, CH), F32),
        ),
        in_specs=[pl.BlockSpec(memory_space=pltpu.SMEM)] * 2 + [vmem] * 4,
        out_specs=(vmem,) * 3,
        scratch_shapes=[
            v((C, EXT)), v((C, EXT)), v((D, RIM)), v((D, 2 * RIM)), v((D, RIM)), v((D, 2 * RIM)),
            v((C, KP)), v((NB, D, BLK), F32), v((NB, D, BLK), F32), v((NSLOT, D, BLK), F32), v((NE, D, BLK), F32),
            v((KP, EXT)), v((KP, EXT)),
            v((C, EXT)), v((C // 2, EXT)), v((C // 2, EXT)), v((2, D, EXT // 2)), v((2, D, EXT)),
            v((D, EXT), F32), v((2, D, RIM), F32), v((2, D, RIM), F32),
            v((C, KP)), v((C, KP)), v((NY - 1, CY, KP)), v((NY - 1, CY, KP)),
            v((NZ, 2 * CH, KW), F32), v((NZ, 2 * CH, KW)), v((NZ, 2 * CH, KW)),
            v((NZ - 1, 2 * CH, KW)), v((NZ - 1, 2 * CH, KW)),
            *dma(28), *dma(2), *dma(28), *dma(2), *dma(2), *dma(6), *dma(2),
            *dma(NY - 1), *dma(NY - 1), *dma(NZ - 1), *dma(NZ - 1),
        ],
        compiler_params=pltpu.CompilerParams(
            collective_id=0, has_side_effects=True, vmem_limit_bytes=56 * 2**20
        ),
    )(index, factor, features, cotangent, weight_one.reshape(KD, C), weight_two.reshape(KD, C))
    return output, one.reshape(K, D, CH), two.reshape(K, D, CH)


def solution(mesh):
    return jax.shard_map(
        local,
        mesh=mesh,
        in_specs=(
            P("space", "chan"),
            P("space", None, None, None),
            P(),
            P(None, "chan", None),
            P(None, "chan", None),
            P("space", "chan"),
        ),
        out_specs=(P("space", "chan"), P(None, "chan", "space"), P(None, "chan", "space")),
        check_vma=False,
    )
```

time: 95.1 us -> 77.5 us (0.81)
  Pallas kernels: 79 us -> 61.1 us
    pallas_call x1, Pallas kernels: 79 us -> 61.1 us  [local(): pl.pallas_call(kernel, out_shape=(jax.ShapeDtypeStruct((OWN, D), BF16), j...]
where the time goes in v2:
time: 77.5 us; the launch traced here: 76.9 us
  Pallas kernels  61.1 us (79%)
  local copies, waits for them, and re-layouts  9.63 us (12%)
  other arithmetic  4.1 us (5%)
  between operations  2.07 us (3%)
    pallas_call x1, Pallas kernels, local(): pl.pallas_call(kernel, out_shape=(jax.ShapeDtypeStruct((OWN, D), BF16), j...  61.1 us
    unnamed x12, local copies, waits for them, and re-layouts  7.36 us
    add x3, other arithmetic, by(): full = key * 512 + number  1.97 us

profile of v2, /device:TPU:1, one launch (start us, length us, event | category | flops | bytes accessed | tf_op | source)
XLA Modules:
  0.0 76.9 jit_solution(11988297659434290141)
XLA Ops:
  0.6 0.0 copy-start.2
  0.6 1.3 %fusion.13 = (s32[1]{0:T(128)}, s32[1]{0:T(128)}) fusion(s32[32]{0:T(128)} %param.8, s32[]{:T(128)S(6)} %max.9, s32[]{:T(128)S(6)} %select_n.128), kind=kLoop, calls=%fused_computation.71 | loop fusion | bytes 24 | tf_op jit(solution)/shard_map/dynamic_slice | solution.py:61
  3.3 0.1 iota_compare_fusion.6
  3.4 0.1 convert_element_type.36
  3.4 0.8 %copy.20 = s32[1,27,16,3]{2,1,3,0:T(8,128)S(1)} copy(s32[1,27,16,3]{1,2,3,0:T(8,128)} %param.7) | data formatting | bytes 10368 | tf_op args[1]
  4.3 0.1 reshape_squeeze.3
  4.4 0.7 iota_add_fusion
  5.1 0.7 iota_add_fusion.2
  5.7 0.3 convert_reduce_fusion.3
  6.0 0.1 convert_reduce_fusion.4
  6.1 0.7 iota_add_fusion.1
  6.8 0.4 convert_reduce_fusion.2
  7.2 0.2 select_reduce_fusion
  7.4 0.1 slice_compare_fusion
  7.5 0.1 slice_compare_fusion.1
  7.5 0.3 convert_reduce_fusion
  7.9 0.1 concatenate.10
  8.0 0.7 concatenate.9.tab
  8.6 0.6 convert_convert_fusion.fac
  9.2 1.9 %copy.21.x_ref = bf16[2048,32]{1,0:T(8,128)(2,1)} copy(bf16[2048,32]{0,1:T(8,128)(2,1)} %param.6) | data formatting | bytes 262144 | tf_op args[0]
  11.1 0.0 copy-done.2
  11.1 1.0 %copy.22.g_ref = bf16[2048,32]{1,0:T(8,128)(2,1)} copy(bf16[2048,32]{0,1:T(8,128)(2,1)S(1)} %copy-done.2) | data formatting | bytes 262144 | tf_op args[5]
  12.2 61.1 %shard_map.85 = (bf16[2048,32]{1,0:T(8,128)(2,1)}, f32[864,8]{1,0:T(8,128)}, f32[864,8]{1,0:T(8,128)}) custom-call(s32[1422]{0:T(1024)} %concatenate.9.tab, f32[1452]{0:T(1024)} %convert_convert_fusion.fac, bf16[2048,32]{1,0:T(8,128)(2,1)} %copy.21.x_ref, bf16[2048,32]{1,0:T(8,128)(2,1)} %copy.22.g_ref, bf16[864,256]{1,0:T(8,128)(2,1)} %bitcast.14, ...), custom_call_target="tpu_custom_call" | custom-call | tf_op jit(solution)/shard_map/pallas_call | solution.py:413
  73.2 0.0 copy-start.1
  73.2 0.0 copy-start
  73.3 2.0 %copy.23 = bf16[2048,32]{0,1:T(8,128)(2,1)} copy(bf16[2048,32]{1,0:T(8,128)(2,1)} %get-tuple-element.15) | data formatting | bytes 262144
  75.2 0.0 copy-done.1
  75.2 0.8 %copy.24 = f32[27,32,8]{1,2,0:T(8,128)} copy(f32[27,32,8]{2,1,0:T(8,128)S(1)} %bitcast.13) | data formatting | bytes 55296
  76.0 0.0 copy-done
  76.0 0.8 %copy.25 = f32[27,32,8]{1,2,0:T(8,128)} copy(f32[27,32,8]{2,1,0:T(8,128)S(1)} %bitcast.12) | data formatting | bytes 55296
  (9 shorter events, 0.1 us)
Async XLA Ops:
  0.6 10.5 %copy-start.2 = (bf16[2048,32]{0,1:T(8,128)(2,1)S(1)}, bf16[2048,32]{0,1:T(8,128)(2,1)}, u32[]{:S(2)}) copy-start(bf16[2048,32]{0,1:T(8,128)(2,1)} %param.11) | copy-start | bytes 393220
  73.2 2.0 %copy-start.1 = (f32[864,8]{1,0:T(8,128)S(1)}, f32[864,8]{1,0:T(8,128)}, u32[]{:S(2)}) copy-start(f32[864,8]{1,0:T(8,128)} %get-tuple-element.7) | copy-start | bytes 82948
  73.2 2.8 %copy-start = (f32[864,8]{1,0:T(8,128)S(1)}, f32[864,8]{1,0:T(8,128)}, u32[]{:S(2)}) copy-start(f32[864,8]{1,0:T(8,128)} %get-tuple-element.8) | copy-start | bytes 82948

commit v3 on v2

--- a/solution.py
+++ b/solution.py
@@ -31,21 +31,13 @@
 F32 = jnp.float32
 BF16 = jnp.bfloat16
 
-T_ROWS = 0
-T_SLOTS = NE
-T_TEND = 2 * NE
-T_SEND = T_TEND + NB
-T_LAST = T_SEND + NSLOT
+NP = 512
+TW = 640
+T_ROWS, T_SLOTS, T_TEND, T_SEND, T_LAST = 0, 1, 2, 3, 4
 
 
 def nt(a, b):
     return lax.dot_general(a, b, (((1,), (1,)), ((), ())), preferred_element_type=F32)
-
-
-def eye(n):
-    row = lax.broadcasted_iota(jnp.int32, (n, n), 0)
-    col = lax.broadcasted_iota(jnp.int32, (n, n), 1)
-    return jnp.where(row == col, 1.0, 0.0).astype(BF16)
 
 
 def by_core():
@@ -55,40 +47,66 @@
     return jnp.where(col == (rest // D) * (2 * D) + core * D + rest % D, 1.0, 0.0).astype(BF16)
 
 
-def tables(kernel_map, block_count):
+def iota(shape, dim):
+    return lax.broadcasted_iota(jnp.int32, shape, dim)
+
+
+def total(cond, axis):
+    return jnp.sum(jnp.where(cond, 1.0, 0.0), axis, keepdims=True)
+
+
+def tables(count_ref, km_ref, index, factor):
     shard = lax.axis_index("space")
-    own = block_count[shard]
-    left = block_count[jnp.maximum(shard - 1, 0)]
-    entries = kernel_map[0].reshape(NE, 3)
-    source, inblock, target = entries[:, 0], entries[:, 1], entries[:, 2]
-    pos = jnp.where(
-        source == shard,
-        inblock,
-        jnp.where(source < shard, NB + inblock - (left - HB), NB + HB + inblock),
-    )
-    live = target < own
-    number = jnp.arange(NE, dtype=jnp.int32)
-    offset = number // EPK
-
-    def by(key, payload, bits, ends):
-        full = key * 512 + number
-        rank = jnp.sum((full[None, :] < full[:, None]).astype(jnp.int32), 1)
-        value = key * bits + payload
-        order = jnp.sum(jnp.where(rank[None, :] == number[:, None], value[None, :], 0), 1)
-        keys = order // bits
-        same = jnp.concatenate([jnp.zeros((1,), jnp.int32), (keys[1:] == keys[:-1]).astype(jnp.int32)])
-        at = jnp.arange(ends, dtype=jnp.int32)[:, None]
-        upto = jnp.sum((key[None, :] <= at).astype(jnp.int32), 1)
-        there = jnp.sum((key[None, :] == at).astype(jnp.int32), 1)
-        return (order % bits, same), (jnp.maximum(upto - 1, 0), (there > 0).astype(jnp.int32))
-
-    rows, tend = by(jnp.where(live, target, NB), pos * K + offset, 1024, NB)
-    slots, send = by(jnp.where(live, offset * NX + pos, NSLOT), target, 32, NSLOT)
-    last = own - HB + jnp.arange(HB, dtype=jnp.int32)
-    which = (last[:, None] == jnp.arange(NB, dtype=jnp.int32)).astype(jnp.int32).reshape(-1)
-    index = jnp.concatenate([rows[0], slots[0], tend[0], send[0], last])
-    factor = jnp.concatenate([rows[1], slots[1], tend[1], send[1], which])
-    return index, factor.astype(F32)
+    own, left = count_ref[shard], count_ref[jnp.maximum(shard - 1, 0)]
+    index[...] = jnp.zeros(index.shape, jnp.int32)
+    factor[...] = jnp.zeros(factor.shape, F32)
+    shard, own, left = shard.astype(F32), own.astype(F32), left.astype(F32)
+    spread = jnp.where((iota((K, NP), 1) & 31) == iota((K, NP), 0), 1.0, 0.0).astype(BF16)
+    gather = jnp.where((iota((NP, K), 0) & 31) == iota((NP, K), 1), 1.0, 0.0).astype(BF16)
+    at_row = (iota((EPK, NP), 1) >> 5) == iota((EPK, NP), 0)
+    at_col = (iota((NP, EPK), 0) >> 5) == iota((NP, EPK), 1)
+
+    def keys(form, axis):
+        shape = (1, NP) if axis == 0 else (NP, 1)
+        number = iota(shape, 1 - axis)
+        offset = number & 31
+        source, inblock, target = (form(km_ref[c].astype(BF16)) for c in range(3))
+        before = NB + inblock - (left - HB)
+        pos = jnp.where(source == shard, inblock, jnp.where(source < shard, before, NB + HB + inblock))
+        pos = jnp.clip(pos, 0.0, NX - 1.0)
+        target = jnp.clip(target, 0.0, NB - 1.0)
+        gone = jnp.maximum(jnp.where(target < own, 0.0, 1.0), jnp.where(offset < K, 0.0, 1.0)) > 0.5
+        known = offset < K
+        offset = offset.astype(F32)
+        by_target = jnp.where(gone, 1.0 * NB, target)
+        by_slot = jnp.where(gone, 1.0 * NSLOT, offset * NX + pos)
+        product = jnp.where(known, pos * K + offset, 0.0)
+        return number.astype(F32), (by_target, by_slot), (product, target)
+
+    def as_row(v):
+        wide = jnp.dot(v, spread, preferred_element_type=F32)
+        return jnp.sum(jnp.where(at_row, wide, 0.0), 0, keepdims=True)
+
+    def as_col(v):
+        return jnp.sum(jnp.where(at_col, nt(gather, v), 0.0), 1, keepdims=True)
+
+    n_row, key_row, _ = keys(as_row, 0)
+    n_col, key_col, pay_col = keys(as_col, 1)
+    for i, width in enumerate((BLK, TW)):
+        key = key_col[i]
+        rank = total(key_row[i] * NP + n_row < key * NP + n_col, 1)
+        sorted_key = jnp.sum(jnp.where(rank == n_row, key, 0.0), 0, keepdims=True)
+        index[i : i + 1, :NP] = jnp.sum(jnp.where(rank == n_row, pay_col[i], 0.0), 0, keepdims=True).astype(jnp.int32)
+        factor[i : i + 1, :NP] = jnp.where(total(key < sorted_key, 0) == n_row, 0.0, 1.0)
+        at = iota((1, width), 1).astype(F32)
+        upto = total(key <= at, 0)
+        index[T_TEND + i : T_TEND + i + 1, :width] = jnp.clip(upto - 1.0, 0.0, NE - 1.0).astype(jnp.int32)
+        factor[T_TEND + i : T_TEND + i + 1, :width] = jnp.minimum(total(key == at, 0), 1.0)
+    block = iota((1, BLK), 1).astype(F32)
+    last = jnp.clip(own - HB + block, 0.0, NB - 1.0)
+    index[T_LAST : T_LAST + 1, :BLK] = last.astype(jnp.int32)
+    for u in range(HB):
+        factor[T_LAST + u : T_LAST + u + 1, :BLK] = jnp.where(block == own - HB + u, 1.0, 0.0)
 
 
 def kernel(
@@ -184,14 +202,11 @@
 
     def load_last(last):
         for u in range(HB):
-            last[:, u * BLK : (u + 1) * BLK] = blocks[tab[T_LAST + u]].astype(BF16)
-
-    ident = eye(D)
-    for b in range(0, NB, 4):
-        four = nt(ident, x_ref[b * BLK : (b + 4) * BLK, :])
-        xall[mine, b * BLK : (b + 4) * BLK] = four.astype(BF16)
-        for u in range(4):
-            blocks[b + u] = four[:, u * BLK : (u + 1) * BLK]
+            last[:, u * BLK : (u + 1) * BLK] = blocks[tab[T_LAST, u]].astype(BF16)
+
+    xall[mine, body] = x_ref[...]
+    for b in range(NB):
+        blocks[b] = x_ref[:, b * BLK : (b + 1) * BLK].astype(F32)
     load_last(xlast)
 
     pl.semaphore_wait(barrier, len(peers))
@@ -206,26 +221,24 @@
         def step(i, total):
             for u in range(8):
                 n = i * 8 + u
-                total = total * fac[base + n] + src[tab[base + n]]
+                total = total * fac[base, n] + src[tab[base, n]]
                 run[n] = total
             return total
 
         lax.fori_loop(0, NE // 8, step, jnp.zeros((D, BLK), F32))
 
-    def run_end(at):
-        return run[tab[at]] * fac[at]
+    def run_end(table, at):
+        return run[tab[table, at]] * fac[table, at]
 
     def fill_slots(dst):
         @pl.loop(0, K)
         def _(k):
             at = pl.ds(pl.multiple_of(k * D, D), D)
             for p in range(NX):
-                dst[at, p * BLK : (p + 1) * BLK] = run_end(T_SEND + k * NX + p).astype(BF16)
-
-    for b in range(0, NB, 4):
-        four = nt(ident, g_ref[b * BLK : (b + 4) * BLK, :])
-        for u in range(4):
-            blocks[b + u] = four[:, u * BLK : (u + 1) * BLK]
+                dst[at, p * BLK : (p + 1) * BLK] = run_end(T_SEND, k * NX + p).astype(BF16)
+
+    for b in range(NB):
+        blocks[b] = g_ref[:, b * BLK : (b + 1) * BLK].astype(F32)
     a_g[KD:, :] = jnp.zeros((KP - KD, EXT), BF16)
     a_z[KD:, :] = jnp.zeros((KP - KD, EXT), BF16)
     w2t[:, KD:] = jnp.zeros((C, KP - KD), BF16)
@@ -292,7 +305,7 @@
     start(to_behind[2])
 
     for b in range(NB):
-        z = run_end(T_TEND + b)
+        z = run_end(T_TEND, b)
         zblk[b] = z
         h = z / (1.0 + jnp.exp(-z))
         blocks[b] = h
@@ -328,7 +341,7 @@
         if b < HB:
             grad = grad + back_in[1, :, b * BLK : (b + 1) * BLK]
         for u in range(HB):
-            grad = grad + back_in[0, :, u * BLK : (u + 1) * BLK] * fac[T_LAST + u * NB + b]
+            grad = grad + back_in[0, :, u * BLK : (u + 1) * BLK] * fac[T_LAST + u, b]
         z = zblk[b]
         gate = 1.0 / (1.0 + jnp.exp(-z))
         grad_z = grad * gate * (1.0 + z * (1.0 - gate))
@@ -378,8 +391,9 @@
             for j, copy in enumerate(self.over_z):
                 copy.wait_recv()
                 total = total + self.zrecv[j].astype(F32)
-            dst[:KW, :] = jnp.transpose(total[:CH, :])
-            dst[KW:, :] = jnp.transpose(total[CH:, :])[: KD - KW, :]
+            for k in range(K):
+                rows, at = (k * D // KW) * CH, k * D % KW
+                dst[k] = total[rows : rows + CH, at : at + D]
 
     one = Sum(ysend1, yrecv1, zsend1, zrecv1, y1s, y1r, z1s, z1r)
     two = Sum(ysend2, yrecv2, zsend2, zrecv2, y2s, y2r, z2s, z2r)
@@ -392,8 +406,8 @@
     two.middle()
     scan(y, T_ROWS)
     for b in range(NB):
-        z = run_end(T_TEND + b)
-        out_ref[b * BLK : (b + 1) * BLK, :] = jnp.transpose(z).astype(BF16)
+        z = run_end(T_TEND, b)
+        out_ref[:, b * BLK : (b + 1) * BLK] = z.astype(BF16)
     one.end(g1_ref)
     two.end(g2_ref)
     for copy in pending:
@@ -401,8 +415,14 @@
 
 
 def local(features, kernel_map, block_count, weight_one, weight_two, cotangent):
-    index, factor = tables(kernel_map, block_count)
     vmem = pl.BlockSpec(memory_space=pltpu.VMEM)
+    smem = pl.BlockSpec(memory_space=pltpu.SMEM)
+    index, factor = pl.pallas_call(
+        tables,
+        out_shape=(jax.ShapeDtypeStruct((8, TW), jnp.int32), jax.ShapeDtypeStruct((8, TW), F32)),
+        in_specs=[smem, vmem],
+        out_specs=(vmem, vmem),
+    )(block_count, kernel_map[0].transpose(2, 1, 0))
 
     def v(shape, kind=BF16):
         return pltpu.VMEM(shape, kind)
@@ -413,11 +433,11 @@
     output, one, two = pl.pallas_call(
         kernel,
         out_shape=(
-            jax.ShapeDtypeStruct((OWN, D), BF16),
-            jax.ShapeDtypeStruct((KD, CH), F32),
-            jax.ShapeDtypeStruct((KD, CH), F32),
+            jax.ShapeDtypeStruct((D, OWN), BF16),
+            jax.ShapeDtypeStruct((K, CH, D), F32),
+            jax.ShapeDtypeStruct((K, CH, D), F32),
         ),
-        in_specs=[pl.BlockSpec(memory_space=pltpu.SMEM)] * 2 + [vmem] * 4,
+        in_specs=[smem] * 2 + [vmem] * 4,
         out_specs=(vmem,) * 3,
         scratch_shapes=[
             v((C, EXT)), v((C, EXT)), v((D, RIM)), v((D, 2 * RIM)), v((D, RIM)), v((D, 2 * RIM)),
@@ -434,8 +454,15 @@
         compiler_params=pltpu.CompilerParams(
             collective_id=0, has_side_effects=True, vmem_limit_bytes=56 * 2**20
         ),
-    )(index, factor, features, cotangent, weight_one.reshape(KD, C), weight_two.reshape(KD, C))
-    return output, one.reshape(K, D, CH), two.reshape(K, D, CH)
+    )(
+        index,
+        factor,
+        features.T,
+        cotangent.T,
+        weight_one.reshape(KD, C),
+        weight_two.reshape(KD, C),
+    )
+    return output.T, one.transpose(0, 2, 1), two.transpose(0, 2, 1)
 
 
 def solution(mesh):

time: 77.5 us -> 69.6 us (0.90)
  local copies, waits for them, and re-layouts: 9.63 us -> 3.19 us
  other arithmetic: 4.1 us -> 0 us
  Pallas kernels: 61.1 us -> 65 us
  between operations: 2.07 us -> 0.65 us
    unnamed x12 -> x7, local copies, waits for them, and re-layouts: 7.36 us -> 3.19 us
    pallas_call x1 -> x2, Pallas kernels: 61.1 us -> 65 us  [the longest x1 61.9 us: local(): pl.pallas_call(kernel, out_shape=(jax.ShapeDtypeStruct((D, OWN), BF16), j...]
    add x5 -> x0, other arithmetic: 1.98 us -> none  [the longest x3 1.97 us: by(): full = key * 512 + number]
    dynamic_slice x1 -> x0, local copies, waits for them, and re-layouts: 1.32 us -> none  [tables(): left = block_count[jnp.maximum(shard - 1, 0)]]
    reduce_sum x5 -> x0, other arithmetic: 1.22 us -> none  [the longest x2 0.61 us: by(): rank = jnp.sum((full[None, :] < full[:, None]).astype(jnp.int32), 1)]
where the time goes in v3:
time: 69.6 us; the launch traced here: 68.8 us
  Pallas kernels  65 us (93%)
  local copies, waits for them, and re-layouts  3.19 us (5%)
    pallas_call x1, Pallas kernels, local(): pl.pallas_call(kernel, out_shape=(jax.ShapeDtypeStruct((D, OWN), BF16), j...  61.9 us
    unnamed x7, local copies, waits for them, and re-layouts  3.19 us
    pallas_call x1, Pallas kernels, local(): pl.pallas_call(tables, out_shape=(jax.ShapeDtypeStruct((8, TW), jnp.int32...  3.08 us

profile of v3, /device:TPU:1, one launch (start us, length us, event | category | flops | bytes accessed | tf_op | source)
XLA Modules:
  0.0 68.8 jit_solution(8088414516724774377)
XLA Ops:
  0.6 3.1 %shard_map.85 = (s32[8,640]{1,0:T(8,128)}, f32[8,640]{1,0:T(8,128)}) custom-call(s32[32]{0:T(128)} %count_ref.1, s32[3,16,27]{2,1,0:T(8,128)} %bitcast.17), custom_call_target="tpu_custom_call" | custom-call | tf_op jit(solution)/shard_map/pallas_call | solution.py:420
  3.7 61.9 %shard_map.86 = (bf16[32,2048]{1,0:T(8,128)(2,1)}, f32[27,8,32]{2,1,0:T(8,128)}, f32[27,8,32]{2,1,0:T(8,128)}) custom-call(s32[8,640]{1,0:T(8,128)} %get-tuple-element.8.tab, f32[8,640]{1,0:T(8,128)} %get-tuple-element.9.fac, bf16[32,2048]{1,0:T(8,128)(2,1)} %bitcast.12, bf16[32,2048]{1,0:T(8,128)(2,1)} %bitcast.13, bf16[864,256]{1,0:T(8,128)(2,1)} %bitcast.10, ...), custom_call_target="tpu_custom_call" | custom-call | tf_op jit(solution)/shard_map/pallas_call | solution.py:433
  65.6 0.0 copy-start.1
  65.6 1.6 %copy.12 = bf16[2048,32]{0,1:T(8,128)(2,1)} copy(bf16[2048,32]{0,1:T(8,128)(2,1)} %bitcast.14) | data formatting | bytes 262144
  67.2 0.0 copy-done.1
  67.3 0.0 copy-start
  67.3 0.6 copy.13
  67.9 0.3 copy-done
  68.2 0.6 copy.14
Async XLA Ops:
  65.6 1.6 %copy-start.1 = (f32[27,8,32]{2,1,0:T(8,128)S(1)}, f32[27,8,32]{2,1,0:T(8,128)}, u32[]{:S(2)}) copy-start(f32[27,8,32]{2,1,0:T(8,128)} %get-tuple-element.11) | copy-start | bytes 82948
  67.3 0.9 %copy-start = (f32[27,8,32]{2,1,0:T(8,128)S(1)}, f32[27,8,32]{2,1,0:T(8,128)}, u32[]{:S(2)}) copy-start(f32[27,8,32]{2,1,0:T(8,128)} %get-tuple-element.12) | copy-start | bytes 82948

commit v4 on v3

--- a/solution.py
+++ b/solution.py
@@ -355,11 +355,13 @@
         def __init__(self, ysend, yrecv, zsend, zrecv, ys, yr, zs, zr):
             self.ysend, self.yrecv, self.zsend, self.zrecv = ysend, yrecv, zsend, zrecv
             self.over_y, self.over_z = [], []
-            for j in range(1, NY):
-                at = pl.ds(pl.multiple_of(lax.rem(row + j, NY) * CY, CY), CY)
-                self.over_y.append(
-                    remote(ysend.at[at], yrecv.at[j - 1], ys.at[j - 1], yr.at[j - 1], (along_y(j), chan))
-                )
+            for i, lanes in enumerate((pl.ds(0, KW), pl.ds(KW, KP - KW))):
+                for j in range(1, NY):
+                    at = pl.ds(pl.multiple_of(lax.rem(row + j, NY) * CY, CY), CY)
+                    n = i * (NY - 1) + j - 1
+                    self.over_y.append(
+                        remote(ysend.at[at, lanes], yrecv.at[j - 1, :, lanes], ys.at[n], yr.at[n], (along_y(j), chan))
+                    )
             for j in range(1, NZ):
                 to = lax.rem(col + j, NZ)
                 self.over_z.append(
@@ -370,8 +372,9 @@
             for n in range(0, KP, 256):
                 at = slice(n, min(n + 256, KP))
                 self.ysend[:, at] = nt(whole[...], a[at, :]).astype(BF16)
-            for copy in self.over_y:
-                start(copy)
+                if at.stop == KW or at.stop == KP:
+                    for copy in self.over_y[: NY - 1] if at.stop == KW else self.over_y[NY - 1 :]:
+                        start(copy)
 
         def middle(self):
             for copy in self.over_y:
@@ -412,6 +415,11 @@
     two.end(g2_ref)
     for copy in pending:
         copy.wait_send()
+
+
+def hand_out(*refs):
+    for src, dst in zip(refs[:3], refs[3:]):
+        dst[...] = src[...]
 
 
 def local(features, kernel_map, block_count, weight_one, weight_two, cotangent):
@@ -449,7 +457,7 @@
             v((NZ, 2 * CH, KW), F32), v((NZ, 2 * CH, KW)), v((NZ, 2 * CH, KW)),
             v((NZ - 1, 2 * CH, KW)), v((NZ - 1, 2 * CH, KW)),
             *dma(28), *dma(2), *dma(28), *dma(2), *dma(2), *dma(6), *dma(2),
-            *dma(NY - 1), *dma(NY - 1), *dma(NZ - 1), *dma(NZ - 1),
+            *dma(2 * NY - 2), *dma(2 * NY - 2), *dma(NZ - 1), *dma(NZ - 1),
         ],
         compiler_params=pltpu.CompilerParams(
             collective_id=0, has_side_effects=True, vmem_limit_bytes=56 * 2**20
@@ -462,6 +470,12 @@
         weight_one.reshape(KD, C),
         weight_two.reshape(KD, C),
     )
+    output, one, two = pl.pallas_call(
+        hand_out,
+        out_shape=tuple(jax.ShapeDtypeStruct(r.shape, r.dtype) for r in (output, one, two)),
+        in_specs=[vmem] * 3,
+        out_specs=(vmem,) * 3,
+    )(output, one, two)
     return output.T, one.transpose(0, 2, 1), two.transpose(0, 2, 1)
 
 

time: 69.6 us -> 67.5 us (0.970)
  local copies, waits for them, and re-layouts: 3.19 us -> 0 us
  Pallas kernels: 65 us -> 66.3 us
    unnamed x7 -> x0, local copies, waits for them, and re-layouts: 3.19 us -> none
    pallas_call x0 -> x1, Pallas kernels: none -> 1.75 us  [local(): pl.pallas_call(hand_out, out_shape=tuple((jax.ShapeDtypeStruct(r.shape, r...]
where the time goes in v4:
time: 67.5 us; the launch traced here: 67 us
  Pallas kernels  66.3 us (98%)
    pallas_call x1, Pallas kernels, local(): pl.pallas_call(kernel, out_shape=(jax.ShapeDtypeStruct((D, OWN), BF16), j...  61.5 us
    pallas_call x1, Pallas kernels, local(): pl.pallas_call(tables, out_shape=(jax.ShapeDtypeStruct((8, TW), jnp.int32...  3.08 us
    pallas_call x1, Pallas kernels, local(): pl.pallas_call(hand_out, out_shape=tuple((jax.ShapeDtypeStruct(r.shape, r...  1.75 us

profile of v4, /device:TPU:1, one launch (start us, length us, event | category | flops | bytes accessed | tf_op | source)
XLA Modules:
  0.0 67.0 jit_solution(4475983432405039175)
XLA Ops:
  0.6 3.1 %shard_map.85 = (s32[8,640]{1,0:T(8,128)}, f32[8,640]{1,0:T(8,128)}) custom-call(s32[32]{0:T(128)} %count_ref.1, s32[3,16,27]{2,1,0:T(8,128)} %bitcast.14), custom_call_target="tpu_custom_call" | custom-call | tf_op jit(solution)/shard_map/pallas_call | solution.py:428
  3.7 61.5 %shard_map.86 = (bf16[32,2048]{1,0:T(8,128)(2,1)}, f32[27,8,32]{2,1,0:T(8,128)}, f32[27,8,32]{2,1,0:T(8,128)}) custom-call(s32[8,640]{1,0:T(8,128)} %get-tuple-element.11.tab, f32[8,640]{1,0:T(8,128)} %get-tuple-element.12.fac, bf16[32,2048]{1,0:T(8,128)(2,1)} %bitcast.12, bf16[32,2048]{1,0:T(8,128)(2,1)} %bitcast.13, bf16[864,256]{1,0:T(8,128)(2,1)} %bitcast.10, ...), custom_call_target="tpu_custom_call" | custom-call | tf_op jit(solution)/shard_map/pallas_call | solution.py:441
  65.2 1.7 %shard_map.87 = (bf16[32,2048]{1,0:T(8,128)(2,1)}, f32[27,8,32]{2,1,0:T(8,128)}, f32[27,8,32]{2,1,0:T(8,128)}) custom-call(bf16[32,2048]{1,0:T(8,128)(2,1)} %get-tuple-element.13.refs_0_, f32[27,8,32]{2,1,0:T(8,128)} %get-tuple-element.14.refs_1_, f32[27,8,32]{2,1,0:T(8,128)} %get-tuple-element.15.refs_2_), custom_call_target="tpu_custom_call" | custom-call | tf_op jit(solution)/shard_map/pallas_call | solution.py:473

commit v5 on v4

--- a/solution.py
+++ b/solution.py
@@ -95,8 +95,9 @@
     for i, width in enumerate((BLK, TW)):
         key = key_col[i]
         rank = total(key_row[i] * NP + n_row < key * NP + n_col, 1)
-        sorted_key = jnp.sum(jnp.where(rank == n_row, key, 0.0), 0, keepdims=True)
-        index[i : i + 1, :NP] = jnp.sum(jnp.where(rank == n_row, pay_col[i], 0.0), 0, keepdims=True).astype(jnp.int32)
+        both = jnp.sum(jnp.where(rank == n_row, key * 1024.0 + pay_col[i], 0.0), 0, keepdims=True).astype(jnp.int32)
+        sorted_key = (both >> 10).astype(F32)
+        index[i : i + 1, :NP] = both & 1023
         factor[i : i + 1, :NP] = jnp.where(total(key < sorted_key, 0) == n_row, 0.0, 1.0)
         at = iota((1, width), 1).astype(F32)
         upto = total(key <= at, 0)

time: 67.5 us -> 67.4 us (level)
  no operation moved by 1% of the time
where the time goes in v5:
time: 67.4 us; the launch traced here: 66.8 us
  Pallas kernels  66.2 us (98%)
    pallas_call x1, Pallas kernels, local(): pl.pallas_call(kernel, out_shape=(jax.ShapeDtypeStruct((D, OWN), BF16), j...  61.5 us
    pallas_call x1, Pallas kernels, local(): pl.pallas_call(tables, out_shape=(jax.ShapeDtypeStruct((8, TW), jnp.int32...  2.95 us
    pallas_call x1, Pallas kernels, local(): pl.pallas_call(hand_out, out_shape=tuple((jax.ShapeDtypeStruct(r.shape, r...  1.75 us

profile of v5, /device:TPU:1, one launch (start us, length us, event | category | flops | bytes accessed | tf_op | source)
XLA Modules:
  0.0 66.8 jit_solution(14851462755757686331)
XLA Ops:
  0.6 3.0 %shard_map.85 = (s32[8,640]{1,0:T(8,128)}, f32[8,640]{1,0:T(8,128)}) custom-call(s32[32]{0:T(128)} %count_ref.1, s32[3,16,27]{2,1,0:T(8,128)} %bitcast.14), custom_call_target="tpu_custom_call" | custom-call | tf_op jit(solution)/shard_map/pallas_call | solution.py:429
  3.6 61.5 %shard_map.86 = (bf16[32,2048]{1,0:T(8,128)(2,1)}, f32[27,8,32]{2,1,0:T(8,128)}, f32[27,8,32]{2,1,0:T(8,128)}) custom-call(s32[8,640]{1,0:T(8,128)} %get-tuple-element.11.tab, f32[8,640]{1,0:T(8,128)} %get-tuple-element.12.fac, bf16[32,2048]{1,0:T(8,128)(2,1)} %bitcast.12, bf16[32,2048]{1,0:T(8,128)(2,1)} %bitcast.13, bf16[864,256]{1,0:T(8,128)(2,1)} %bitcast.10, ...), custom_call_target="tpu_custom_call" | custom-call | tf_op jit(solution)/shard_map/pallas_call | solution.py:442
  65.1 1.7 %shard_map.87 = (bf16[32,2048]{1,0:T(8,128)(2,1)}, f32[27,8,32]{2,1,0:T(8,128)}, f32[27,8,32]{2,1,0:T(8,128)}) custom-call(bf16[32,2048]{1,0:T(8,128)(2,1)} %get-tuple-element.13.refs_0_, f32[27,8,32]{2,1,0:T(8,128)} %get-tuple-element.14.refs_1_, f32[27,8,32]{2,1,0:T(8,128)} %get-tuple-element.15.refs_2_), custom_call_target="tpu_custom_call" | custom-call | tf_op jit(solution)/shard_map/pallas_call | solution.py:474
